TPU v7x, 128 devices: a whole 4x4x4 slice. The times are simulated.
128 devices in a mesh: wide: 32 (over x, z, core), narrow: 4 (over y).
Axes of the slice: x: 4, y: 4, z: 4, core: 2. Of those that a mesh axis runs over, the one named last changes fastest.
Arguments:
- front: bfloat16 [4, 32, 128, 32, 4, 128], P(None, 'wide', None, None, 'narrow'), may hold values from -6 to 6
- pivot_inverse: bfloat16 [4, 128, 128], replicated, may hold values from -0.0105112052 to 0.17838107
- rhs: bfloat16 [4, 32, 128, 256], P(None, 'wide'), may hold values from -6 to 6
- trail_sol: bfloat16 [4, 32, 128, 256], P(None, 'wide'), may hold values from -1.1953125 to 1.1953125
- block_mask: int32 [4, 32, 32, 4], P(None, 'wide', None, 'narrow'), may hold values 0 or 1
- panel_order: int32 [4], replicated, may hold values from 0 to 3, each once
Outputs:
- front_out: bfloat16 [4, 32, 128, 32, 4, 128], P(None, 'wide', None, None, 'narrow')
- forward_rhs: bfloat16 [4, 32, 128, 256], P(None, 'wide')
- window_solution: bfloat16 [4, 128, 256], replicated
Inputs may be any that keep to these rules, and one draw needn't show every extreme that they name: `panel_order`: each value 0 to 3 appears once.
All inputs are finite; a program needn't handle non-finite values. No bound on the sum of `block_mask` on one device may be relied on, other than what follows from the above.
Results may differ from a plain program's by a relative error of at most 0.0076.
Values may be sent and summed in bfloat16 or wider, within the bound.
No kernel may reach another device: no remote copies, remote signals or barrier semaphores. Data moves between devices by JAX's collectives and lax.ppermute only.
A program may use at most 64 MiB of HBM per device.

v0:
```python
import jax
import jax.numpy as jnp
from jax import lax
from jax.sharding import PartitionSpec as P


def spread(block, axis, source):
    block = jnp.where(lax.axis_index(axis) == source, block, jnp.zeros_like(block))
    return lax.psum(block, axis)


def body(front, pivot_inverse, rhs, trail_sol, block_mask, panel_order):
    rloc = front.shape[0]
    bsize = front.shape[2]
    cloc = front.shape[3]
    nrhs_local = rhs.shape[3]
    panels = panel_order.shape[0]
    nwide = lax.axis_size("wide")
    nnarrow = lax.axis_size("narrow")
    blocks = front.reshape(rloc, bsize, cloc, bsize)
    pattern = block_mask.reshape(rloc, cloc).astype(jnp.float32)
    right = rhs.reshape(rloc, bsize, nrhs_local)
    rows_global = jnp.arange(rloc, dtype=jnp.int32) * nwide + lax.axis_index("wide")
    cols_global = jnp.arange(cloc, dtype=jnp.int32) * nnarrow + lax.axis_index("narrow")
    section_ids = jnp.arange(panels, dtype=jnp.int32)
    rows_rank = jnp.min(
        jnp.where(rows_global[:, None] == panel_order[None, :], section_ids[None, :], panels),
        axis=1,
    )
    cols_rank = jnp.min(
        jnp.where(cols_global[:, None] == panel_order[None, :], section_ids[None, :], panels),
        axis=1,
    )

    def pivot_weight(target):
        return lax.dynamic_index_in_dim(pivot_inverse, target, 0, keepdims=False)

    def panel_factors(col_blocks, row_blocks, target, section):
        weight = pivot_weight(target)
        left = jnp.einsum("rab,bc->rac", col_blocks, weight, preferred_element_type=jnp.float32)
        left = jnp.where((rows_rank > section)[:, None, None], left, 0.0).astype(jnp.bfloat16)
        left = spread(left, "narrow", target % nnarrow)
        upper = jnp.einsum("ac,ajb->cjb", weight, row_blocks, preferred_element_type=jnp.float32)
        upper = jnp.where((cols_rank > section)[None, :, None], upper, 0.0).astype(jnp.bfloat16)
        upper = spread(upper, "wide", target % nwide)
        return (left, upper)

    def column_of(current, target):
        return lax.dynamic_index_in_dim(current, target // nnarrow, 2, keepdims=False)

    def row_of(current, target):
        return lax.dynamic_index_in_dim(current, target // nwide, 0, keepdims=False)

    saved_left = []
    saved_pivot = []
    left, upper = panel_factors(
        column_of(blocks, panel_order[0]), row_of(blocks, panel_order[0]), panel_order[0], 0
    )
    for section in range(panels):
        target = panel_order[section]
        weight = pivot_weight(target)
        product = jnp.einsum("rac,cjb->rajb", left, upper, preferred_element_type=jnp.float32)
        blocks = (blocks.astype(jnp.float32) - pattern[:, None, :, None] * product).astype(
            jnp.bfloat16
        )
        if section + 1 < panels:
            following = panel_order[section + 1]
            next_left, next_upper = panel_factors(
                column_of(blocks, following), row_of(blocks, following), following, section + 1
            )
        pivot_rhs = lax.dynamic_index_in_dim(right, target // nwide, 0, keepdims=False)
        solved = jnp.einsum(
            "ac,an->cn", weight, pivot_rhs, preferred_element_type=jnp.float32
        ).astype(jnp.bfloat16)
        solved = spread(solved, "wide", target % nwide)
        elimination = jnp.einsum("rac,cn->ran", left, solved, preferred_element_type=jnp.float32)
        right = (right.astype(jnp.float32) - elimination).astype(jnp.bfloat16)
        saved_left.append(left)
        saved_pivot.append(solved)
        if section + 1 < panels:
            left, upper = (next_left, next_upper)
    current = trail_sol.reshape(rloc, bsize, nrhs_local)
    window = jnp.zeros((panels, bsize, nrhs_local), jnp.bfloat16)
    for section in reversed(range(panels)):
        target = panel_order[section]
        partial_sum = jnp.einsum(
            "rac,ran->cn", saved_left[section], current, preferred_element_type=jnp.float32
        )
        total = lax.psum(partial_sum, "wide")
        corrected = (saved_pivot[section].astype(jnp.float32) - total).astype(jnp.bfloat16)
        result = jnp.einsum(
            "ac,cn->an", pivot_weight(target), corrected, preferred_element_type=jnp.float32
        ).astype(jnp.bfloat16)
        current = jnp.where((rows_global == target)[:, None, None], result[None], current)
        window = lax.dynamic_update_index_in_dim(window, result, target, 0)
    return (blocks.reshape(front.shape), right.reshape(rhs.shape), window)


def solution(mesh):
    in_specs = (
        P(None, "wide", None, None, "narrow", None),
        P(),
        P(None, "wide", None, None),
        P(None, "wide", None, None),
        P(None, "wide", None, "narrow"),
        P(),
    )
    out_specs = (P(None, "wide", None, None, "narrow", None), P(None, "wide", None, None), P())
    return jax.shard_map(body, mesh=mesh, in_specs=in_specs, out_specs=out_specs, check_vma=False)
```

profile of v0, /device:TPU:1, one launch (start us, length us, event | category | flops | bytes accessed | tf_op | source)
XLA Modules:
  0.0 1070.7 jit_solution(9461470469571352421)
XLA Ops:
  7.2 1.5 fusion.111
  13.5 1.5 constant_dynamic-slice_fusion.1
  16.0 1.3 constant_dynamic-slice_fusion
  18.1 1.6 fusion.2
  24.1 34.5 %all-reduce.17.cloned.1.call-done = bf16[4,128,128]{2,1,0:T(8,128)(2,1)} async-done(((bf16[4,128,128]{2,1,0:T(8,128)(2,1)}), bf16[4,128,128]{2,1,0:T(8,128)(2,1)}) %all-reduce.17.cloned.1.call-update) | async-done | bytes 131088 | tf_op jit(solution)/shard_map/psum | solution.py:9
  58.6 112.0 %all-reduce.39.cloned.1.call-done = (bf16[128,32,128]{2,0,1:T(8,128)(2,1)}, bf16[128,256]{1,0:T(8,128)(2,1)}) async-done(((bf16[128,32,128]{2,0,1:T(8,128)(2,1)}, bf16[128,256]{1,0:T(8,128)(2,1)}), (bf16[128,32,128]{2,0,1:T(8,128)(2,1)}, bf16[128,256]{1,0:T(8,128)(2,1)})) %all-reduce.39.cloned.1.call-update) | async-done | bytes 1114128 | tf_op jit(solution)/shard_map/psum | solution.py:9
  170.6 4.7 fusion
  175.3 2.0 copy-done.2
  178.2 2.7 fusion.3
  185.6 31.7 %all-reduce.19.cloned.1.call-done = bf16[4,128,128]{2,1,0:T(8,128)(2,1)} async-done(((bf16[4,128,128]{2,1,0:T(8,128)(2,1)}), bf16[4,128,128]{2,1,0:T(8,128)(2,1)}) %all-reduce.19.cloned.1.call-update) | async-done | bytes 131088 | tf_op jit(solution)/shard_map/psum | solution.py:9
  217.3 111.8 %all-reduce.37.cloned.1.call-done = (bf16[128,32,128]{2,0,1:T(8,128)(2,1)}, bf16[128,256]{1,0:T(8,128)(2,1)}) async-done(((bf16[128,32,128]{2,0,1:T(8,128)(2,1)}, bf16[128,256]{1,0:T(8,128)(2,1)}), (bf16[128,32,128]{2,0,1:T(8,128)(2,1)}, bf16[128,256]{1,0:T(8,128)(2,1)})) %all-reduce.37.cloned.1.call-update) | async-done | bytes 1114128 | tf_op jit(solution)/shard_map/psum | solution.py:9
  329.1 3.8 subtract_convert_fusion.2
  333.0 2.0 copy-done.1
  335.9 2.7 fusion.4
  343.9 31.0 %all-reduce.21.cloned.1.call-done = bf16[4,128,128]{2,1,0:T(8,128)(2,1)} async-done(((bf16[4,128,128]{2,1,0:T(8,128)(2,1)}), bf16[4,128,128]{2,1,0:T(8,128)(2,1)}) %all-reduce.21.cloned.1.call-update) | async-done | bytes 131088 | tf_op jit(solution)/shard_map/psum | solution.py:9
  374.9 111.8 %all-reduce.35.cloned.1.call-done = (bf16[128,32,128]{2,0,1:T(8,128)(2,1)}, bf16[128,256]{1,0:T(8,128)(2,1)}) async-done(((bf16[128,32,128]{2,0,1:T(8,128)(2,1)}, bf16[128,256]{1,0:T(8,128)(2,1)}), (bf16[128,32,128]{2,0,1:T(8,128)(2,1)}, bf16[128,256]{1,0:T(8,128)(2,1)})) %all-reduce.35.cloned.1.call-update) | async-done | bytes 1114128 | tf_op jit(solution)/shard_map/psum | solution.py:9
  486.7 3.8 subtract_convert_fusion.1
  490.6 2.0 copy-done.3
  493.5 2.7 fusion.5
  496.4 36.1 %all-reduce.23.cloned.1.call-done = bf16[4,128,128]{2,1,0:T(8,128)(2,1)} async-done(((bf16[4,128,128]{2,1,0:T(8,128)(2,1)}), bf16[4,128,128]{2,1,0:T(8,128)(2,1)}) %all-reduce.23.cloned.1.call-update) | async-done | bytes 131088 | tf_op jit(solution)/shard_map/psum | solution.py:9
  532.5 1.9 convolution_bitcast_fusion.3
  536.7 103.3 %all-reduce.25.cloned.1.call-done = f32[128,256]{1,0:T(8,128)} async-done(((f32[128,256]{1,0:T(8,128)}), f32[128,256]{1,0:T(8,128)}) %all-reduce.25.cloned.1.call-update) | async-done | bytes 131088 | tf_op jit(solution)/shard_map/psum | solution.py:89
  639.9 109.0 %all-reduce.33.cloned.1.call-done = (bf16[128,32,128]{2,0,1:T(8,128)(2,1)}, bf16[128,256]{1,0:T(8,128)(2,1)}) async-done(((bf16[128,32,128]{2,0,1:T(8,128)(2,1)}, bf16[128,256]{1,0:T(8,128)(2,1)}), (bf16[128,32,128]{2,0,1:T(8,128)(2,1)}, bf16[128,256]{1,0:T(8,128)(2,1)})) %all-reduce.33.cloned.1.call-update) | async-done | bytes 1114128 | tf_op jit(solution)/shard_map/psum | solution.py:9
  749.0 1.1 bitcast_dynamic-update-slice_fusion.2
  751.6 101.7 %all-reduce.27.cloned.1.call-done = f32[128,256]{1,0:T(8,128)} async-done(((f32[128,256]{1,0:T(8,128)}), f32[128,256]{1,0:T(8,128)}) %all-reduce.27.cloned.1.call-update) | async-done | bytes 131088 | tf_op jit(solution)/shard_map/psum | solution.py:89
  853.3 1.1 bitcast_dynamic-update-slice_fusion.1
  855.5 5.7 fusion.1
  861.3 96.5 %all-reduce.29.cloned.1.call-done = f32[128,256]{1,0:T(8,128)} async-done(((f32[128,256]{1,0:T(8,128)}), f32[128,256]{1,0:T(8,128)}) %all-reduce.29.cloned.1.call-update) | async-done | bytes 131088 | tf_op jit(solution)/shard_map/psum | solution.py:89
  957.7 1.1 bitcast_dynamic-update-slice_fusion
  960.7 6.9 copy.30
  967.6 94.5 %all-reduce.31.cloned.1.call-done = f32[128,256]{1,0:T(8,128)} async-done(((f32[128,256]{1,0:T(8,128)}), f32[128,256]{1,0:T(8,128)}) %all-reduce.31.cloned.1.call-update) | async-done | bytes 131088 | tf_op jit(solution)/shard_map/psum | solution.py:89
  1062.1 1.0 fusion.24
  (79 shorter events, 16.1 us)
Async XLA Ops:
  7.2 7.9 copy-start
  7.2 12.5 %copy-start.9 = (bf16[4,1,128,256]{3,2,1,0:T(8,128)(2,1)S(1)}, bf16[4,1,128,256]{3,2,1,0:T(8,128)(2,1)}, u32[]{:S(2)}) copy-start(bf16[4,1,128,256]{3,2,1,0:T(8,128)(2,1)} %param.8) | copy-start | bytes 786436
  7.2 16.3 %copy-start.15 = (s32[4,1,32,1]{2,3,1,0:T(1,128)S(1)}, s32[4,1,32,1]{2,3,1,0:T(1,128)}, u32[]{:S(2)}) copy-start(s32[4,1,32,1]{2,3,1,0:T(1,128)} %param.10) | copy-start | bytes 1540
  7.2 51.4 %all-reduce.17.cloned.1.call-start = ((), (), s32[]{:S(2)}) async-start(), calls=%async_computation | async-start | bytes 262144 | tf_op jit(solution)/shard_map/psum | solution.py:9
  15.9 154.7 %all-reduce.39.cloned.1.call-start = ((), (), s32[]{:S(2)}) async-start(), calls=%async_computation.11 | async-start | bytes 2228224 | tf_op jit(solution)/shard_map/psum | solution.py:9
  20.5 196.7 %all-reduce.19.cloned.1.call-start = ((), (), s32[]{:S(2)}) async-start(), calls=%async_computation.1 | async-start | bytes 262144 | tf_op jit(solution)/shard_map/psum | solution.py:9
  170.6 10.3 copy-start.7
  170.6 10.3 copy-start.11
  175.3 2.0 copy-start.2
  178.2 150.9 %all-reduce.37.cloned.1.call-start = ((), (), s32[]{:S(2)}) async-start(), calls=%async_computation.10 | async-start | bytes 2228224 | tf_op jit(solution)/shard_map/psum | solution.py:9
  182.0 192.9 %all-reduce.21.cloned.1.call-start = ((), (), s32[]{:S(2)}) async-start(), calls=%async_computation.2 | async-start | bytes 262144 | tf_op jit(solution)/shard_map/psum | solution.py:9
  329.1 9.5 copy-start.8
  329.1 9.5 copy-start.12
  333.0 2.0 copy-start.1
  335.8 150.9 %all-reduce.35.cloned.1.call-start = ((), (), s32[]{:S(2)}) async-start(), calls=%async_computation.9 | async-start | bytes 2228224 | tf_op jit(solution)/shard_map/psum | solution.py:9
  339.6 192.9 %all-reduce.23.cloned.1.call-start = ((), (), s32[]{:S(2)}) async-start(), calls=%async_computation.3 | async-start | bytes 262144 | tf_op jit(solution)/shard_map/psum | solution.py:9
  486.7 9.5 copy-start.4
  486.7 9.5 copy-start.13
  486.7 45.8 %copy-start.6 = (bf16[4,1,128,256]{3,2,1,0:T(8,128)(2,1)S(1)}, bf16[4,1,128,256]{3,2,1,0:T(8,128)(2,1)}, u32[]{:S(2)}) copy-start(bf16[4,1,128,256]{3,2,1,0:T(8,128)(2,1)} %param.9) | copy-start | bytes 786436
  490.6 2.0 copy-start.3
  493.5 146.5 %all-reduce.25.cloned.1.call-start = ((), (), s32[]{:S(2)}) async-start(), calls=%async_computation.4 | async-start | bytes 262144 | tf_op jit(solution)/shard_map/psum | solution.py:89
  532.5 323.0 %copy-start.5 = (bf16[4,128,128]{2,1,0:T(8,128)(2,1)S(1)}, bf16[4,128,128]{2,1,0:T(8,128)(2,1)}, u32[]{:S(2)}) copy-start(bf16[4,128,128]{2,1,0:T(8,128)(2,1)} %all-reduce.23.cloned.1.call-done) | copy-start | bytes 393220
  534.4 214.5 %all-reduce.33.cloned.1.call-start = ((), (), s32[]{:S(2)}) async-start(), calls=%async_computation.8 | async-start | bytes 2228224 | tf_op jit(solution)/shard_map/psum | solution.py:9
  535.3 318.0 %all-reduce.27.cloned.1.call-start = ((), (), s32[]{:S(2)}) async-start(), calls=%async_computation.5 | async-start | bytes 262144 | tf_op jit(solution)/shard_map/psum | solution.py:89
  751.0 206.8 %all-reduce.29.cloned.1.call-start = ((), (), s32[]{:S(2)}) async-start(), calls=%async_computation.6 | async-start | bytes 262144 | tf_op jit(solution)/shard_map/psum | solution.py:89
  855.3 206.8 %all-reduce.31.cloned.1.call-start = ((), (), s32[]{:S(2)}) async-start(), calls=%async_computation.7 | async-start | bytes 262144 | tf_op jit(solution)/shard_map/psum | solution.py:89
  855.5 104.2 %copy-start.14 = (bf16[128,256]{1,0:T(8,128)(2,1)S(1)}, bf16[128,256]{1,0:T(8,128)(2,1)}, u32[]{:S(2)}) copy-start(bf16[128,256]{1,0:T(8,128)(2,1)} %get-tuple-element.13) | copy-start | bytes 196612
  1063.1 0.7 copy-start.10
Sparse Core Ops, SparseCore 0:
  16.0 42.5 all-reduce.16
  62.7 107.9 all-reduce.38
  178.3 38.9 all-reduce.18
  221.1 107.9 all-reduce.36
  335.9 38.8 all-reduce.20
  378.8 107.9 all-reduce.34
  493.6 38.8 all-reduce.22
  536.3 103.5 all-reduce.24
  644.0 104.9 all-reduce.32
  752.6 100.6 all-reduce.26
  857.1 100.6 all-reduce.28
  961.4 100.6 all-reduce.30
where the time goes:
time: 1070 us
  waiting for transfers between devices  974 us (91%)
  matrix products  44.8 us (4%)
  between operations  29.6 us (3%)
  local copies, waits for them, and re-layouts  18 us (2%)
    psum x8, waiting for transfers between devices, spread(): return lax.psum(block, axis)  578 us
    psum x4, waiting for transfers between devices, body(): total = lax.psum(partial_sum, 'wide')  396 us
  transfers between devices with their start and end apart: 12, of which 12 were waited for; matrix products, arithmetic and copies ran while one was open for 3% of the time, Pallas kernels for 0%

commit v1 on v0

--- a/solution.py
+++ b/solution.py
@@ -86,7 +86,13 @@
         partial_sum = jnp.einsum(
             "rac,ran->cn", saved_left[section], current, preferred_element_type=jnp.float32
         )
-        total = lax.psum(partial_sum, "wide")
+        total, a_next = (partial_sum, 0)
+        world = lax.axis_size("wide")
+        while 1 << a_next < world:
+            carry_out = tuple(((to_i, to_i ^ 1 << a_next) for to_i in range(world)))
+            out_arr = lax.ppermute(total, axis_name="wide", perm=carry_out)
+            total = total + out_arr
+            a_next = a_next + 1
         corrected = (saved_pivot[section].astype(jnp.float32) - total).astype(jnp.bfloat16)
         result = jnp.einsum(
             "ac,cn->an", pivot_weight(target), corrected, preferred_element_type=jnp.float32

time: 1070 us -> 737 us (0.69)
  waiting for transfers between devices: 974 us -> 607 us
  starting transfers between devices: 0.68 us -> 42.5 us
    psum x4 -> x0, waiting for transfers between devices: 396 us -> none  [body(): total = lax.psum(partial_sum, 'wide')]
    ppermute x0 -> x20, waiting for transfers between devices: none -> 47.5 us  [body(): out_arr = lax.ppermute(total, axis_name='wide', perm=carry_out)]
    ppermute x0 -> x20, starting transfers between devices: none -> 42.2 us  [body(): out_arr = lax.ppermute(total, axis_name='wide', perm=carry_out)]
    psum x8, waiting for transfers between devices: 578 us -> 560 us  [spread(): return lax.psum(block, axis)]
  transfers between devices with their start and end apart: 12 -> 28, of which waited for: 12 -> 26; matrix products, arithmetic and copies ran while one was open for 3% -> 3% of each run, Pallas kernels for 0% -> 0%
where the time goes in v1:
time: 737 us; the launch traced here: 734 us
  waiting for transfers between devices  607 us (82%)
  starting transfers between devices  42.5 us (6%)
  matrix products  35.1 us (5%)
  between operations  29.4 us (4%)
  local copies, waits for them, and re-layouts  15.8 us (2%)
    psum x8, waiting for transfers between devices, spread(): return lax.psum(block, axis)  560 us
    ppermute x20, waiting for transfers between devices, body(): out_arr = lax.ppermute(total, axis_name='wide', perm=carry_out)  47.5 us
    ppermute x20, starting transfers between devices, body(): out_arr = lax.ppermute(total, axis_name='wide', perm=carry_out)  42.2 us
  transfers between devices with their start and end apart: 28, of which 26 were waited for; matrix products, arithmetic and copies ran while one was open for 3% of the time, Pallas kernels for 0%

profile of v1, /device:TPU:1, one launch (start us, length us, event | category | flops | bytes accessed | tf_op | source)
XLA Modules:
  0.0 733.9 jit_solution(11264260198025887327)
XLA Ops:
  24.1 34.5 %all-reduce.13.cloned.1.call-done = bf16[4,128,128]{2,1,0:T(8,128)(2,1)} async-done(((bf16[4,128,128]{2,1,0:T(8,128)(2,1)}), bf16[4,128,128]{2,1,0:T(8,128)(2,1)}) %all-reduce.13.cloned.1.call-update) | async-done | bytes 131088 | tf_op jit(solution)/shard_map/psum | solution.py:9
  58.6 112.0 %all-reduce.27.cloned.1.call-done = (bf16[128,32,128]{2,0,1:T(8,128)(2,1)}, bf16[128,256]{1,0:T(8,128)(2,1)}) async-done(((bf16[128,32,128]{2,0,1:T(8,128)(2,1)}, bf16[128,256]{1,0:T(8,128)(2,1)}), (bf16[128,32,128]{2,0,1:T(8,128)(2,1)}, bf16[128,256]{1,0:T(8,128)(2,1)})) %all-reduce.27.cloned.1.call-update) | async-done | bytes 1114128 | tf_op jit(solution)/shard_map/psum | solution.py:9
  170.6 4.7 fusion
  178.2 2.7 fusion.3
  185.4 31.9 %all-reduce.15.cloned.1.call-done = bf16[4,128,128]{2,1,0:T(8,128)(2,1)} async-done(((bf16[4,128,128]{2,1,0:T(8,128)(2,1)}), bf16[4,128,128]{2,1,0:T(8,128)(2,1)}) %all-reduce.15.cloned.1.call-update) | async-done | bytes 131088 | tf_op jit(solution)/shard_map/psum | solution.py:9
  217.3 111.8 %all-reduce.25.cloned.1.call-done = (bf16[128,32,128]{2,0,1:T(8,128)(2,1)}, bf16[128,256]{1,0:T(8,128)(2,1)}) async-done(((bf16[128,32,128]{2,0,1:T(8,128)(2,1)}, bf16[128,256]{1,0:T(8,128)(2,1)}), (bf16[128,32,128]{2,0,1:T(8,128)(2,1)}, bf16[128,256]{1,0:T(8,128)(2,1)})) %all-reduce.25.cloned.1.call-update) | async-done | bytes 1114128 | tf_op jit(solution)/shard_map/psum | solution.py:9
  329.1 3.8 subtract_convert_fusion.2
  335.9 2.7 fusion.4
  343.8 31.1 %all-reduce.17.cloned.1.call-done = bf16[4,128,128]{2,1,0:T(8,128)(2,1)} async-done(((bf16[4,128,128]{2,1,0:T(8,128)(2,1)}), bf16[4,128,128]{2,1,0:T(8,128)(2,1)}) %all-reduce.17.cloned.1.call-update) | async-done | bytes 131088 | tf_op jit(solution)/shard_map/psum | solution.py:9
  374.9 111.8 %all-reduce.23.cloned.1.call-done = (bf16[128,32,128]{2,0,1:T(8,128)(2,1)}, bf16[128,256]{1,0:T(8,128)(2,1)}) async-done(((bf16[128,32,128]{2,0,1:T(8,128)(2,1)}, bf16[128,256]{1,0:T(8,128)(2,1)}), (bf16[128,32,128]{2,0,1:T(8,128)(2,1)}, bf16[128,256]{1,0:T(8,128)(2,1)})) %all-reduce.23.cloned.1.call-update) | async-done | bytes 1114128 | tf_op jit(solution)/shard_map/psum | solution.py:9
  486.7 3.8 subtract_convert_fusion.1
  496.4 36.1 %all-reduce.19.cloned.1.call-done = bf16[4,128,128]{2,1,0:T(8,128)(2,1)} async-done(((bf16[4,128,128]{2,1,0:T(8,128)(2,1)}), bf16[4,128,128]{2,1,0:T(8,128)(2,1)}) %all-reduce.19.cloned.1.call-update) | async-done | bytes 131088 | tf_op jit(solution)/shard_map/psum | solution.py:9
  533.6 2.8 collective-permute-start
  538.8 3.4 collective-permute-done.1
  542.3 2.9 collective-permute-start.2
  551.6 3.2 collective-permute-start.4
  555.5 90.5 %all-reduce.21.cloned.1.call-done = (bf16[128,32,128]{2,0,1:T(8,128)(2,1)}, bf16[128,256]{1,0:T(8,128)(2,1)}) async-done(((bf16[128,32,128]{2,0,1:T(8,128)(2,1)}, bf16[128,256]{1,0:T(8,128)(2,1)}), (bf16[128,32,128]{2,0,1:T(8,128)(2,1)}, bf16[128,256]{1,0:T(8,128)(2,1)})) %all-reduce.21.cloned.1.call-update) | async-done | bytes 1114128 | tf_op jit(solution)/shard_map/psum | solution.py:9
  649.6 4.2 collective-permute-done.6
  653.8 2.7 collective-permute-start.7
  660.0 3.1 collective-permute-done.8
  663.2 3.2 collective-permute-start.9
  666.9 3.0 collective-permute-done.9
  670.4 3.7 collective-permute-start.10
  675.5 4.4 collective-permute-done.11
  682.2 3.2 collective-permute-done.12
  689.4 3.9 collective-permute-start.14
  693.9 2.8 collective-permute-done.14
  697.2 3.7 collective-permute-start.15
  702.2 4.5 collective-permute-done.16
  707.9 4.2 collective-permute-done.17
  715.1 4.7 copy.38
  719.9 3.9 collective-permute-start.19
  (127 shorter events, 59.2 us)
Async XLA Ops:
  7.2 51.4 %all-reduce.13.cloned.1.call-start = ((), (), s32[]{:S(2)}) async-start(), calls=%async_computation | async-start | bytes 262144 | tf_op jit(solution)/shard_map/psum | solution.py:9
  15.9 154.7 %all-reduce.27.cloned.1.call-start = ((), (), s32[]{:S(2)}) async-start(), calls=%async_computation.7 | async-start | bytes 2228224 | tf_op jit(solution)/shard_map/psum | solution.py:9
  20.5 196.7 %all-reduce.15.cloned.1.call-start = ((), (), s32[]{:S(2)}) async-start(), calls=%async_computation.1 | async-start | bytes 262144 | tf_op jit(solution)/shard_map/psum | solution.py:9
  178.2 150.9 %all-reduce.25.cloned.1.call-start = ((), (), s32[]{:S(2)}) async-start(), calls=%async_computation.6 | async-start | bytes 2228224 | tf_op jit(solution)/shard_map/psum | solution.py:9
  182.0 192.9 %all-reduce.17.cloned.1.call-start = ((), (), s32[]{:S(2)}) async-start(), calls=%async_computation.2 | async-start | bytes 262144 | tf_op jit(solution)/shard_map/psum | solution.py:9
  335.8 150.9 %all-reduce.23.cloned.1.call-start = ((), (), s32[]{:S(2)}) async-start(), calls=%async_computation.5 | async-start | bytes 2228224 | tf_op jit(solution)/shard_map/psum | solution.py:9
  339.7 192.9 %all-reduce.19.cloned.1.call-start = ((), (), s32[]{:S(2)}) async-start(), calls=%async_computation.3 | async-start | bytes 262144 | tf_op jit(solution)/shard_map/psum | solution.py:9
  486.7 45.8 %copy-start.7 = (bf16[4,1,128,256]{3,2,1,0:T(8,128)(2,1)S(1)}, bf16[4,1,128,256]{3,2,1,0:T(8,128)(2,1)}, u32[]{:S(2)}) copy-start(bf16[4,1,128,256]{3,2,1,0:T(8,128)(2,1)} %param.9) | copy-start | bytes 786436
  493.4 152.5 %all-reduce.21.cloned.1.call-start = ((), (), s32[]{:S(2)}) async-start(), calls=%async_computation.4 | async-start | bytes 2228224 | tf_op jit(solution)/shard_map/psum | solution.py:9
  533.6 3.8 collective-permute-start
  537.5 4.8 collective-permute-start.1
  542.3 5.4 collective-permute-start.2
  547.7 3.9 collective-permute-start.3
  551.6 94.3 %collective-permute-start.4 = (f32[128,256]{1,0:T(8,128)S(1)}, f32[128,256]{1,0:T(8,128)S(1)}, u32[]{:S(2)}, u32[]{:S(2)}) collective-permute-start(f32[128,256]{1,0:T(8,128)S(1)} %add.235), channel_id=1, source_target_pairs={{0,64},{4,68},{8,72},{12,76},{16,80},{20,84},{24,88},{28,92},{32,9... | collective-permute-start | bytes 393224 | tf_op jit(solution)/shard_map/ppermute | solution.py:93
  646.0 67.8 %copy-start.2 = (bf16[4,128,32,128]{3,1,2,0:T(8,128)(2,1)S(1)}, bf16[4,128,32,128]{3,1,2,0:T(8,128)(2,1)}, u32[]{:S(2)}) copy-start(bf16[4,128,32,128]{3,1,2,0:T(8,128)(2,1)} %copy-done.1) | copy-start | bytes 12582916
  646.0 67.8 %copy-start.5 = (bf16[4,128,128]{2,1,0:T(8,128)(2,1)S(1)}, bf16[4,128,128]{2,1,0:T(8,128)(2,1)}, u32[]{:S(2)}) copy-start(bf16[4,128,128]{2,1,0:T(8,128)(2,1)} %all-reduce.19.cloned.1.call-done) | copy-start | bytes 393220
  646.0 67.8 %copy-start.8 = (bf16[128,32,128]{2,0,1:T(8,128)(2,1)S(1)}, bf16[128,32,128]{2,0,1:T(8,128)(2,1)}, u32[]{:S(2)}) copy-start(bf16[128,32,128]{2,0,1:T(8,128)(2,1)} %get-tuple-element.12) | copy-start | bytes 3145732
  647.4 1.6 collective-permute-start.5
  649.0 4.8 collective-permute-start.6
  653.8 5.4 collective-permute-start.7
  659.2 3.9 collective-permute-start.8
  663.2 6.8 collective-permute-start.9
  670.4 4.7 collective-permute-start.10
  675.1 4.8 collective-permute-start.11
  679.9 5.4 collective-permute-start.12
  685.3 4.0 collective-permute-start.13
  689.4 7.3 collective-permute-start.14
  697.2 4.7 collective-permute-start.15
  701.9 4.8 collective-permute-start.16
  706.7 5.4 collective-permute-start.17
  712.1 7.7 %collective-permute-start.18 = (f32[128,256]{1,0:T(8,128)S(1)}, f32[128,256]{1,0:T(8,128)S(1)}, u32[]{:S(2)}, u32[]{:S(2)}) collective-permute-start(f32[128,256]{1,0:T(8,128)S(1)} %add.249), channel_id=1, source_target_pairs={{0,32},{4,36},{8,40},{12,44},{16,48},{20,52},{24,56},{28,60},{32,0... | collective-permute-start | bytes 393224 | tf_op jit(solution)/shard_map/ppermute | solution.py:93
  719.9 6.3 collective-permute-start.19
  (14 other events, 110.5 us)
Sparse Core Ops, SparseCore 0:
  16.0 42.5 all-reduce.12
  62.6 107.9 all-reduce.26
  178.3 38.9 all-reduce.14
  221.1 107.9 all-reduce.24
  335.9 38.8 all-reduce.16
  378.7 107.9 all-reduce.22
  493.6 38.8 all-reduce.18
  537.4 108.4 all-reduce.20
